TPU v7x, 32 devices: a whole 2x2x4 slice. The times are simulated.
32 devices in a mesh: row: 4 (over x, core), col: 8 (over z, y).
Axes of the slice: x: 2, y: 2, z: 4, core: 2. Of those that a mesh axis runs over, the one named last changes fastest.
Arguments:
- item_ids: int32 [8192], P(('row', 'col')), may hold values from 0 to 63
- user_lengths: int32 [8], replicated, may hold values from 1 to 2048, 8192 in all
- catalogue: bfloat16 [64, 1024], P(('row', 'col')), may hold values from -6 to 6
- tap_lengths: int32 [1, 1024], replicated, may hold values from 64 to 256
- conv_taps: bfloat16 [1, 256, 1024], replicated, may hold values from -0.375 to 0.375
- norm_gains: float32 [1, 2, 1024], replicated, may hold values from 0.1 to 1.9
- gate_weight: bfloat16 [1, 1024, 1024], P(None, 'col'), may hold values from -0.1875 to 0.1875
- up_weight: bfloat16 [1, 1024, 1024], P(None, 'col'), may hold values from -0.1875 to 0.1875
- down_weight: bfloat16 [1, 1024, 1024], P(None, 'col'), may hold values from -0.1875 to 0.1875
Outputs:
- history_out: bfloat16 [8192, 1024], P(('row', 'col'))
Inputs may be any that keep to these rules, and one draw needn't show every extreme that they name: `user_lengths`: the 8 lengths sum to 8192.
All inputs are finite; a program needn't handle non-finite values.
Results may differ from a plain program's by a relative error of at most 0.0054.
Values may be sent and summed in bfloat16 or wider, within the bound.
No kernel may reach another device: no remote copies, remote signals or barrier semaphores. Data moves between devices by JAX's collectives and lax.ppermute only.
A program may use at most 64 MiB of HBM per device.

v0:
```python
import jax
import jax.numpy as jnp
from jax import lax
from jax.sharding import PartitionSpec as P

epsilon = 1e-06
group_taps = 32


def from_behind(block, axis, distance):
    devices = range(lax.axis_size(axis))
    route = [(i - distance, i) for i in devices if i - distance in devices]
    return lax.ppermute(block, axis, route)


def rms_norm(values, gains):
    scale = lax.rsqrt(jnp.mean(values * values, axis=-1, keepdims=True) + epsilon)
    return values * scale * gains


def token_ages(positions, user_starts):
    reached = user_starts[None, :] <= positions[:, None]
    fallback = jnp.minimum(positions, 0)[:, None]
    seg_start = jnp.max(jnp.where(reached, user_starts[None, :], fallback), axis=1)
    return positions - seg_start


def earlier_items(item_ids, wanted):
    current = item_ids
    pieces = []
    current = from_behind(current, ("row", "col"), 1)
    pieces = [current] + pieces
    return pieces[0][-wanted:]


def convolve(extended, tap_table, token_age, out_rows):
    reach = extended.shape[0] - out_rows
    groups = -(-tap_table.shape[0] // group_taps)

    def one_group(group_index, accumulated):
        for within in range(group_taps):
            lag_index = group_index * group_taps + within
            shifted = lax.dynamic_slice_in_dim(extended, reach - lag_index, out_rows, 0)
            weights = lax.dynamic_slice_in_dim(tap_table, lag_index, 1, 0)
            keep = (lag_index <= token_age)[:, None]
            accumulated = accumulated + jnp.where(keep, shifted * weights, 0.0)
        return accumulated

    blank = jnp.zeros((out_rows, extended.shape[1]), jnp.float32)
    return lax.fori_loop(0, groups, one_group, blank)


def feed_forward(hidden, gains_row, gate_rows, up_rows, down_rows):
    inner = rms_norm(hidden, gains_row).astype(jnp.bfloat16)
    columns = inner
    first_sum = jnp.dot(
        columns,
        lax.all_gather(gate_rows, "col", axis=0, tiled=True),
        preferred_element_type=jnp.float32,
    )
    second_sum = jnp.dot(
        columns,
        lax.all_gather(up_rows, "col", axis=0, tiled=True),
        preferred_element_type=jnp.float32,
    )
    activated = (jax.nn.silu(first_sum) * second_sum).astype(jnp.bfloat16)
    columns = activated
    projected = jnp.dot(
        columns,
        lax.all_gather(down_rows, "col", axis=0, tiled=True),
        preferred_element_type=jnp.float32,
    )
    return hidden + projected


def body(
    item_ids,
    user_lengths,
    catalogue,
    tap_lengths,
    conv_taps,
    norm_gains,
    gate_weight,
    up_weight,
    down_weight,
):
    row_count = item_ids.shape[0]
    reach = conv_taps.shape[1] - 1
    layer_count = conv_taps.shape[0]
    catalogue_all = lax.all_gather(catalogue, ("row", "col"), axis=0, tiled=True)
    device_index = lax.axis_index("row") * lax.axis_size("col") + lax.axis_index("col")
    first_row = device_index * row_count
    user_starts = jnp.cumsum(user_lengths) - user_lengths
    lag_column = jnp.arange(conv_taps.shape[1], dtype=jnp.int32)[:, None]
    tap_tables = conv_taps.astype(jnp.float32) * (
        lag_column[None] < tap_lengths[:, None, :]
    ).astype(jnp.float32)
    extra = reach * layer_count
    wide_ids = jnp.concatenate([earlier_items(item_ids, extra), item_ids], axis=0)
    hidden = jnp.take(catalogue_all, wide_ids, axis=0).astype(jnp.float32)
    positions = first_row - extra + jnp.arange(row_count + extra, dtype=jnp.int32)
    all_ages = token_ages(positions, user_starts)
    out_rows = row_count + reach * (layer_count - 1)
    normed = rms_norm(hidden, norm_gains[0, 0]).astype(jnp.bfloat16)
    hidden = hidden[-out_rows:] + convolve(normed, tap_tables[0], all_ages[-out_rows:], out_rows)
    hidden = feed_forward(hidden, norm_gains[0, 1], gate_weight[0], up_weight[0], down_weight[0])
    return hidden.astype(jnp.bfloat16)


def solution(mesh):
    return jax.shard_map(
        body,
        mesh=mesh,
        in_specs=(
            P(("row", "col")),
            P(),
            P(("row", "col"), None),
            P(),
            P(),
            P(),
            P(None, "col", None),
            P(None, "col", None),
            P(None, "col", None),
        ),
        out_specs=P(("row", "col"), None),
        check_vma=False,
    )
```

profile of v0, /device:TPU:2, one launch (start us, length us, event | category | flops | bytes accessed | tf_op | source)
XLA Modules:
  0.0 230.7 jit_solution(10582264455192001664)
XLA Ops:
  8.1 3.4 %collective-permute-start = (s32[256]{0:T(256)}, s32[256]{0:T(256)S(1)}, u32[]{:S(2)}, u32[]{:S(2)}) collective-permute-start(s32[256]{0:T(256)} %param.11), channel_id=1, source_target_pairs={{0,1},{1,2},{2,3},{3,4},{4,5},{5,6},{6,7},{7,8},{8,9},{9,10},{10,1... | collective-permute-start | bytes 3080 | tf_op jit(solution)/shard_map/ppermute | solution.py:13
  13.9 2.2 select_bitcast_fusion
  16.1 69.4 %all-gather.3 = bf16[32,2,1024]{2,1,0:T(2,128)(2,1)S(1)} all-gather(bf16[1,2,1024]{2,1,0:T(2,128)(2,1)S(1)} %bitcast.163), channel_id=1, replica_groups=mesh['row'=4,'col'=8] {'row','col'}, dimensions={0}, use_global_device_ids=true | all-gather | bytes 135168 | tf_op jit(solution)/shard_map/all_gather | solution.py:90
  85.9 2.1 gather_fusion
  88.8 124.7 %while.17 = (s32[]{:T(128)}, f32[256,1024]{1,0:T(8,128)S(1)}, s32[256]{0:T(256)S(1)}, bf16[511,1024]{1,0:T(8,128)(2,1)S(1)}, f32[256,1024]{1,0:T(8,128)}, /*inde...) while((s32[]{:T(128)}, f32[256,1024]{1,0:T(8,128)S(1)}, ...), condition=%wide.region_4.5_spmd.clone, body=%wide.region_3.4_spmd.clone.sunk | while | flops 33825024 | bytes 19289948 | solution.py:50
  88.9 1.5 constant_dynamic-slice_fusion.35
  90.5 1.4 constant_dynamic-slice_fusion.34
  92.3 12.3 %select_add_fusion.3 = f32[256,1024]{1,0:T(8,128)S(1)} fusion(f32[256,1024]{1,0:T(8,128)S(1)} %get-tuple-element.605, f32[1024]{0:T(1024)S(1)} %bitcast.128, bf16[511,1024]{1,0:T(8,128)(2,1)S(1)} %get-tuple-element.679, s32[]{:T(128)S(6)} %select_n.1373, f32[1024]{0:T(1024)S(1)} %bitcast.129, s32[]{:T(128)S(6)} %select_n.1374, ...), kind=kLoop, calls=%fused_computation.26.clone.1 | loop fusion | flops 33816576 | bytes 19013760 | tf_op jit(solution)/shard_map/while/body/eval_jaxpr/add | solution.py:46
  106.1 1.4 constant_dynamic-slice_fusion.34
  107.8 12.3 %select_add_fusion.3 = f32[256,1024]{1,0:T(8,128)S(1)} fusion(f32[256,1024]{1,0:T(8,128)S(1)} %get-tuple-element.605, f32[1024]{0:T(1024)S(1)} %bitcast.128, bf16[511,1024]{1,0:T(8,128)(2,1)S(1)} %get-tuple-element.679, s32[]{:T(128)S(6)} %select_n.1373, f32[1024]{0:T(1024)S(1)} %bitcast.129, s32[]{:T(128)S(6)} %select_n.1374, ...), kind=kLoop, calls=%fused_computation.26.clone.1 | loop fusion | flops 33816576 | bytes 19013760 | tf_op jit(solution)/shard_map/while/body/eval_jaxpr/add | solution.py:46
  121.6 1.4 constant_dynamic-slice_fusion.34
  123.4 12.3 %select_add_fusion.3 = f32[256,1024]{1,0:T(8,128)S(1)} fusion(f32[256,1024]{1,0:T(8,128)S(1)} %get-tuple-element.605, f32[1024]{0:T(1024)S(1)} %bitcast.128, bf16[511,1024]{1,0:T(8,128)(2,1)S(1)} %get-tuple-element.679, s32[]{:T(128)S(6)} %select_n.1373, f32[1024]{0:T(1024)S(1)} %bitcast.129, s32[]{:T(128)S(6)} %select_n.1374, ...), kind=kLoop, calls=%fused_computation.26.clone.1 | loop fusion | flops 33816576 | bytes 19013760 | tf_op jit(solution)/shard_map/while/body/eval_jaxpr/add | solution.py:46
  137.2 1.4 constant_dynamic-slice_fusion.34
  138.9 12.3 %select_add_fusion.3 = f32[256,1024]{1,0:T(8,128)S(1)} fusion(f32[256,1024]{1,0:T(8,128)S(1)} %get-tuple-element.605, f32[1024]{0:T(1024)S(1)} %bitcast.128, bf16[511,1024]{1,0:T(8,128)(2,1)S(1)} %get-tuple-element.679, s32[]{:T(128)S(6)} %select_n.1373, f32[1024]{0:T(1024)S(1)} %bitcast.129, s32[]{:T(128)S(6)} %select_n.1374, ...), kind=kLoop, calls=%fused_computation.26.clone.1 | loop fusion | flops 33816576 | bytes 19013760 | tf_op jit(solution)/shard_map/while/body/eval_jaxpr/add | solution.py:46
  152.7 1.4 constant_dynamic-slice_fusion.34
  154.5 12.3 %select_add_fusion.3 = f32[256,1024]{1,0:T(8,128)S(1)} fusion(f32[256,1024]{1,0:T(8,128)S(1)} %get-tuple-element.605, f32[1024]{0:T(1024)S(1)} %bitcast.128, bf16[511,1024]{1,0:T(8,128)(2,1)S(1)} %get-tuple-element.679, s32[]{:T(128)S(6)} %select_n.1373, f32[1024]{0:T(1024)S(1)} %bitcast.129, s32[]{:T(128)S(6)} %select_n.1374, ...), kind=kLoop, calls=%fused_computation.26.clone.1 | loop fusion | flops 33816576 | bytes 19013760 | tf_op jit(solution)/shard_map/while/body/eval_jaxpr/add | solution.py:46
  168.3 1.4 constant_dynamic-slice_fusion.34
  170.0 12.3 %select_add_fusion.3 = f32[256,1024]{1,0:T(8,128)S(1)} fusion(f32[256,1024]{1,0:T(8,128)S(1)} %get-tuple-element.605, f32[1024]{0:T(1024)S(1)} %bitcast.128, bf16[511,1024]{1,0:T(8,128)(2,1)S(1)} %get-tuple-element.679, s32[]{:T(128)S(6)} %select_n.1373, f32[1024]{0:T(1024)S(1)} %bitcast.129, s32[]{:T(128)S(6)} %select_n.1374, ...), kind=kLoop, calls=%fused_computation.26.clone.1 | loop fusion | flops 33816576 | bytes 19013760 | tf_op jit(solution)/shard_map/while/body/eval_jaxpr/add | solution.py:46
  183.8 1.4 constant_dynamic-slice_fusion.34
  185.6 12.3 %select_add_fusion.3 = f32[256,1024]{1,0:T(8,128)S(1)} fusion(f32[256,1024]{1,0:T(8,128)S(1)} %get-tuple-element.605, f32[1024]{0:T(1024)S(1)} %bitcast.128, bf16[511,1024]{1,0:T(8,128)(2,1)S(1)} %get-tuple-element.679, s32[]{:T(128)S(6)} %select_n.1373, f32[1024]{0:T(1024)S(1)} %bitcast.129, s32[]{:T(128)S(6)} %select_n.1374, ...), kind=kLoop, calls=%fused_computation.26.clone.1 | loop fusion | flops 33816576 | bytes 19013760 | tf_op jit(solution)/shard_map/while/body/eval_jaxpr/add | solution.py:46
  199.4 1.4 constant_dynamic-slice_fusion.34
  201.2 12.3 %select_add_fusion.3 = f32[256,1024]{1,0:T(8,128)S(1)} fusion(f32[256,1024]{1,0:T(8,128)S(1)} %get-tuple-element.605, f32[1024]{0:T(1024)S(1)} %bitcast.128, bf16[511,1024]{1,0:T(8,128)(2,1)S(1)} %get-tuple-element.679, s32[]{:T(128)S(6)} %select_n.1373, f32[1024]{0:T(1024)S(1)} %bitcast.129, s32[]{:T(128)S(6)} %select_n.1374, ...), kind=kLoop, calls=%fused_computation.26.clone.1 | loop fusion | flops 33816576 | bytes 19013760 | tf_op jit(solution)/shard_map/while/body/eval_jaxpr/add | solution.py:46
  215.4 3.9 %fusion.28 = f32[256,1024]{1,0:T(8,128)} fusion(bf16[1,1024,1024]{2,1,0:T(8,128)(2,1)} %all-gather.8.cloned.1.call-done, f32[1024]{0:T(1024)S(1)} %bitcast.165, f32[256]{0:T(256)S(1)} %add_rsqrt_fusion.1, f32[256,1024]{1,0:T(8,128)S(1)} %get-tuple-element.276, f32[511,1024]{1,0:T(8,128)} %copy-done), kind=kOutput, calls=%fused_computation.95 | convolution fusion | flops 537919488 | bytes 5248000 | tf_op jit(solution)/shard_map/dot_general | solution.py:56
  219.3 4.9 %fusion.36 = bf16[256,1024]{1,0:T(8,128)(2,1)} fusion(bf16[1,1024,1024]{2,1,0:T(8,128)(2,1)} %all-gather.12.cloned.1.call-done, bf16[1,1024,1024]{2,1,0:T(8,128)(2,1)} %all-gather.10.cloned.1.call-done, f32[256,1024]{1,0:T(8,128)} %fusion.28, f32[1024]{0:T(1024)S(1)} %bitcast.166, f32[256]{0:T(256)S(1)} %add_rsqrt_fusion.1, ...), kind=kOutput, calls=%fused_computation.101 | convolution fusion | flops 1077149696 | bytes 9966592 | tf_op jit(solution)/shard_map/dot_general | solution.py:68
  (60 shorter events, 16.1 us)
Async XLA Ops:
  6.5 79.2 %copy-start.3 = (s32[256]{0:T(256)S(1)}, s32[256]{0:T(256)}, u32[]{:S(2)}) copy-start(s32[256]{0:T(256)} %param.11) | copy-start | bytes 3076
  6.5 9.6 %copy-start.2 = (bf16[2,1024]{1,0:T(2,128)(2,1)S(1)}, bf16[2,1024]{1,0:T(2,128)(2,1)}, u32[]{:S(2)}) copy-start(bf16[2,1024]{1,0:T(2,128)(2,1)} %param.13) | copy-start | bytes 12292
  6.5 208.8 %all-gather.8.cloned.1.call-start = ((), (), s32[]{:S(2)}) async-start(), calls=%async_computation | async-start | bytes 2359296 | tf_op jit(solution)/shard_map/all_gather | solution.py:58
  7.3 212.0 %all-gather.10.cloned.1.call-start = ((), (), s32[]{:S(2)}) async-start(), calls=%async_computation.1 | async-start | bytes 2359296 | tf_op jit(solution)/shard_map/all_gather | solution.py:63
  8.0 211.3 %all-gather.12.cloned.1.call-start = ((), (), s32[]{:S(2)}) async-start(), calls=%async_computation.2 | async-start | bytes 2359296 | tf_op jit(solution)/shard_map/all_gather | solution.py:70
  8.1 77.6 %collective-permute-start = (s32[256]{0:T(256)}, s32[256]{0:T(256)S(1)}, u32[]{:S(2)}, u32[]{:S(2)}) collective-permute-start(s32[256]{0:T(256)} %param.11), channel_id=1, source_target_pairs={{0,1},{1,2},{2,3},{3,4},{4,5},{5,6},{6,7},{7,8},{8,9},{9,10},{10,1... | collective-permute-start | bytes 3080 | tf_op jit(solution)/shard_map/ppermute | solution.py:13
  213.7 1.4 copy-start
  215.4 3.9 %copy-start.1 = (f32[511,1024]{1,0:T(8,128)S(1)}, f32[511,1024]{1,0:T(8,128)}, u32[]{:S(2)}) copy-start(f32[511,1024]{1,0:T(8,128)} %copy-done) | copy-start | bytes 6279172
Sparse Core Ops, SparseCore 0:
  9.5 50.3 all-gather.7
  62.0 48.4 all-gather.9
  112.6 47.6 all-gather.11
where the time goes:
time: 233 us; the launch traced here: 231 us
  other arithmetic  104 us (45%)
  blocking collectives  69.4 us (30%)
  local copies, waits for them, and re-layouts  25.8 us (11%)
  between operations  13.2 us (6%)
  matrix products  8.77 us (4%)
  loops' own time  4.23 us (2%)
  starting transfers between devices  3.51 us (2%)
    add x8, other arithmetic, one_group(): accumulated = accumulated + jnp.where(keep, shifted * weights, 0.0)  98.5 us
    all_gather x1, blocking collectives, body(): lax.all_gather(catalogue, ('row', 'col'), axis=0, tiled=True)  69.4 us
    dynamic_slice x16, local copies, waits for them, and re-layouts, one_group(): weights = lax.dynamic_slice_in_dim(tap_table, lag_index, 1, 0)  21.4 us
    dot_general x1, matrix products, feed_forward(): jnp.dot(columns, lax.all_gather(down_rows, 'col', axis=0, tiled=True), pr...  4.87 us
  transfers between devices with their start and end apart: 4, of which 0 were waited for; matrix products, arithmetic and copies ran while one was open for 57% of the time, Pallas kernels for 0%

commit v1 on v0

--- a/solution.py
+++ b/solution.py
@@ -87,7 +87,16 @@
     row_count = item_ids.shape[0]
     reach = conv_taps.shape[1] - 1
     layer_count = conv_taps.shape[0]
-    catalogue_all = lax.all_gather(catalogue, ("row", "col"), axis=0, tiled=True)
+    ways, here = (lax.axis_size(("row", "col")), lax.axis_index(("row", "col")))
+    catalogue_all, reach_2 = (catalogue, 1)
+    while reach_2 < ways:
+        theirs = lax.ppermute(
+            catalogue_all, ("row", "col"), [(d, d ^ reach_2) for d in range(ways)]
+        )
+        mine_first = jnp.concatenate([catalogue_all, theirs], axis=0)
+        theirs_first = jnp.concatenate([theirs, catalogue_all], axis=0)
+        catalogue_all = jnp.where(here & reach_2 == 0, mine_first, theirs_first)
+        reach_2 = 2 * reach_2
     device_index = lax.axis_index("row") * lax.axis_size("col") + lax.axis_index("col")
     first_row = device_index * row_count
     user_starts = jnp.cumsum(user_lengths) - user_lengths

time: 233 us -> 181 us (0.78)
  blocking collectives: 69.4 us -> 0 us
  waiting for transfers between devices: 1.45 us -> 10.5 us
  starting transfers between devices: 3.51 us -> 9.03 us
    all_gather x1 -> x0, blocking collectives: 69.4 us -> none  [body(): lax.all_gather(catalogue, ('row', 'col'), axis=0, tiled=True)]
    ppermute x0 -> x5, waiting for transfers between devices: none -> 9.07 us  [body(): lax.ppermute(catalogue_all, ('row', 'col'), [(d, d ^ reach_2) for d in ra...]
    ppermute x0 -> x5, starting transfers between devices: none -> 6.55 us  [body(): lax.ppermute(catalogue_all, ('row', 'col'), [(d, d ^ reach_2) for d in ra...]
  transfers between devices with their start and end apart: 4 -> 9, of which waited for: 0 -> 4; matrix products, arithmetic and copies ran while one was open for 57% -> 76% of each run, Pallas kernels for 0% -> 0%
where the time goes in v1:
time: 181 us; the launch traced here: 178 us
  other arithmetic  104 us (57%)
  local copies, waits for them, and re-layouts  27.7 us (15%)
  between operations  13.3 us (7%)
  waiting for transfers between devices  10.5 us (6%)
  starting transfers between devices  9.03 us (5%)
  matrix products  8.78 us (5%)
  loops' own time  4.24 us (2%)
    add x8, other arithmetic, one_group(): accumulated = accumulated + jnp.where(keep, shifted * weights, 0.0)  98.5 us
    dynamic_slice x16, local copies, waits for them, and re-layouts, one_group(): weights = lax.dynamic_slice_in_dim(tap_table, lag_index, 1, 0)  23.3 us
    ppermute x5, waiting for transfers between devices, body(): lax.ppermute(catalogue_all, ('row', 'col'), [(d, d ^ reach_2) for d in ra...  9.07 us
    ppermute x5, starting transfers between devices, body(): lax.ppermute(catalogue_all, ('row', 'col'), [(d, d ^ reach_2) for d in ra...  6.55 us
    dot_general x1, matrix products, feed_forward(): jnp.dot(columns, lax.all_gather(down_rows, 'col', axis=0, tiled=True), pr...  4.88 us
    another operation x1, loops' own time, convolve(): return lax.fori_loop(0, groups, one_group, blank)  4.24 us
    dot_general x1, matrix products, feed_forward(): jnp.dot(columns, lax.all_gather(gate_rows, 'col', axis=0, tiled=True), pr...  3.9 us
  transfers between devices with their start and end apart: 9, of which 4 were waited for; matrix products, arithmetic and copies ran while one was open for 76% of the time, Pallas kernels for 0%

profile of v1, /device:TPU:2, one launch (start us, length us, event | category | flops | bytes accessed | tf_op | source)
XLA Modules:
  0.0 177.9 jit_solution(8969971401221011926)
XLA Ops:
  8.1 1.6 collective-permute-start.1
  9.6 2.4 %collective-permute-start = (s32[256]{0:T(256)}, s32[256]{0:T(256)S(1)}, u32[]{:S(2)}, u32[]{:S(2)}) collective-permute-start(s32[256]{0:T(256)} %param.11), channel_id=1, source_target_pairs={{0,1},{1,2},{2,3},{3,4},{4,5},{5,6},{6,7},{7,8},{8,9},{9,10},{10,1... | collective-permute-start | bytes 3080 | tf_op jit(solution)/shard_map/ppermute | solution.py:13
  14.4 2.2 %select_bitcast_fusion = f32[256,1024]{1,0:T(8,128)} fusion(bf16[1,256,1024]{2,1,0:T(8,128)(2,1)} %param.15, s32[1024]{0:T(1024)} %bitcast.161), kind=kLoop, calls=%fused_computation.106 | loop fusion | flops 786432 | bytes 1576960 | tf_op jit(solution)/shard_map/squeeze | solution.py:114
  16.7 1.6 collective-permute-start.2
  18.5 1.9 %collective-permute-done.2 = bf16[4,1024]{1,0:T(4,128)(2,1)S(1)} collective-permute-done((bf16[4,1024]{1,0:T(4,128)(2,1)S(1)}, bf16[4,1024]{1,0:T(4,128)(2,1)S(1)}, u32[]{:S(2)}, u32[]{:S(2)}) %collective-permute-start.2) | collective-permute-done | bytes 8224 | tf_op jit(solution)/shard_map/ppermute | solution.py:93
  20.5 2.7 %collective-permute-start.3 = (bf16[8,1024]{1,0:T(8,128)(2,1)S(1)}, bf16[8,1024]{1,0:T(8,128)(2,1)S(1)}, u32[]{:S(2)}, u32[]{:S(2)}) collective-permute-start(bf16[8,1024]{1,0:T(8,128)(2,1)S(1)} %maximum_select_fusion.3), channel_id=1, source_target_pairs={{0,4},{1,5},{2,6},{3,7},{4,0},{5,1},{6,2},{7,3},{8,12},{9,13},{10,... | collective-permute-start | bytes 49160 | tf_op jit(solution)/shard_map/ppermute | solution.py:93
  23.2 2.3 %collective-permute-done.3 = bf16[8,1024]{1,0:T(8,128)(2,1)S(1)} collective-permute-done((bf16[8,1024]{1,0:T(8,128)(2,1)S(1)}, bf16[8,1024]{1,0:T(8,128)(2,1)S(1)}, u32[]{:S(2)}, u32[]{:S(2)}) %collective-permute-start.3) | collective-permute-done | bytes 16416 | tf_op jit(solution)/shard_map/ppermute | solution.py:93
  27.5 3.6 %collective-permute-done.5 = bf16[32,1024]{1,0:T(8,128)(2,1)S(1)} collective-permute-done((bf16[32,1024]{1,0:T(8,128)(2,1)S(1)}, bf16[32,1024]{1,0:T(8,128)(2,1)S(1)}, u32[]{:S(2)}, u32[]{:S(2)}) %collective-permute-start.5) | collective-permute-done | bytes 65568 | tf_op jit(solution)/shard_map/ppermute | solution.py:93
  31.2 2.1 %gather_fusion = bf16[511,1024]{1,0:T(8,128)(2,1)S(1)} fusion(bf16[64,1024]{1,0:T(8,128)(2,1)S(1)} %maximum_select_fusion, s32[1024]{0:T(1024)S(1)} %pad_clamp_fusion), kind=kCustom, calls=%fused_computation | custom fusion | bytes 2095100 | tf_op jit(solution)/shard_map/jit(_take)/gather | solution.py:109
  34.1 126.6 %while.17 = (s32[]{:T(128)}, f32[256,1024]{1,0:T(8,128)S(1)}, s32[256]{0:T(256)S(1)}, bf16[511,1024]{1,0:T(8,128)(2,1)S(1)}, f32[256,1024]{1,0:T(8,128)}, /*inde...) while((s32[]{:T(128)}, f32[256,1024]{1,0:T(8,128)S(1)}, ...), condition=%wide.region_4.5_spmd.clone, body=%wide.region_3.4_spmd.clone.sunk | while | flops 33825024 | bytes 19289948 | solution.py:50
  35.7 1.6 constant_dynamic-slice_fusion.34
  37.7 12.3 %select_add_fusion.3 = f32[256,1024]{1,0:T(8,128)S(1)} fusion(f32[256,1024]{1,0:T(8,128)S(1)} %get-tuple-element.605, f32[1024]{0:T(1024)S(1)} %bitcast.127, bf16[511,1024]{1,0:T(8,128)(2,1)S(1)} %get-tuple-element.679, s32[]{:T(128)S(6)} %select_n.1433, f32[1024]{0:T(1024)S(1)} %bitcast.128, s32[]{:T(128)S(6)} %select_n.1434, ...), kind=kLoop, calls=%fused_computation.26.clone.1 | loop fusion | flops 33816576 | bytes 19013760 | tf_op jit(solution)/shard_map/while/body/eval_jaxpr/add | solution.py:46
  51.7 1.6 constant_dynamic-slice_fusion.34
  53.7 12.3 %select_add_fusion.3 = f32[256,1024]{1,0:T(8,128)S(1)} fusion(f32[256,1024]{1,0:T(8,128)S(1)} %get-tuple-element.605, f32[1024]{0:T(1024)S(1)} %bitcast.127, bf16[511,1024]{1,0:T(8,128)(2,1)S(1)} %get-tuple-element.679, s32[]{:T(128)S(6)} %select_n.1433, f32[1024]{0:T(1024)S(1)} %bitcast.128, s32[]{:T(128)S(6)} %select_n.1434, ...), kind=kLoop, calls=%fused_computation.26.clone.1 | loop fusion | flops 33816576 | bytes 19013760 | tf_op jit(solution)/shard_map/while/body/eval_jaxpr/add | solution.py:46
  67.5 1.7 constant_dynamic-slice_fusion.34
  69.5 12.3 %select_add_fusion.3 = f32[256,1024]{1,0:T(8,128)S(1)} fusion(f32[256,1024]{1,0:T(8,128)S(1)} %get-tuple-element.605, f32[1024]{0:T(1024)S(1)} %bitcast.127, bf16[511,1024]{1,0:T(8,128)(2,1)S(1)} %get-tuple-element.679, s32[]{:T(128)S(6)} %select_n.1433, f32[1024]{0:T(1024)S(1)} %bitcast.128, s32[]{:T(128)S(6)} %select_n.1434, ...), kind=kLoop, calls=%fused_computation.26.clone.1 | loop fusion | flops 33816576 | bytes 19013760 | tf_op jit(solution)/shard_map/while/body/eval_jaxpr/add | solution.py:46
  82.0 1.5 constant_dynamic-slice_fusion.35
  85.3 12.3 %select_add_fusion.3 = f32[256,1024]{1,0:T(8,128)S(1)} fusion(f32[256,1024]{1,0:T(8,128)S(1)} %get-tuple-element.605, f32[1024]{0:T(1024)S(1)} %bitcast.127, bf16[511,1024]{1,0:T(8,128)(2,1)S(1)} %get-tuple-element.679, s32[]{:T(128)S(6)} %select_n.1433, f32[1024]{0:T(1024)S(1)} %bitcast.128, s32[]{:T(128)S(6)} %select_n.1434, ...), kind=kLoop, calls=%fused_computation.26.clone.1 | loop fusion | flops 33816576 | bytes 19013760 | tf_op jit(solution)/shard_map/while/body/eval_jaxpr/add | solution.py:46
  101.1 12.3 %select_add_fusion.3 = f32[256,1024]{1,0:T(8,128)S(1)} fusion(f32[256,1024]{1,0:T(8,128)S(1)} %get-tuple-element.605, f32[1024]{0:T(1024)S(1)} %bitcast.127, bf16[511,1024]{1,0:T(8,128)(2,1)S(1)} %get-tuple-element.679, s32[]{:T(128)S(6)} %select_n.1433, f32[1024]{0:T(1024)S(1)} %bitcast.128, s32[]{:T(128)S(6)} %select_n.1434, ...), kind=kLoop, calls=%fused_computation.26.clone.1 | loop fusion | flops 33816576 | bytes 19013760 | tf_op jit(solution)/shard_map/while/body/eval_jaxpr/add | solution.py:46
  116.9 12.3 %select_add_fusion.3 = f32[256,1024]{1,0:T(8,128)S(1)} fusion(f32[256,1024]{1,0:T(8,128)S(1)} %get-tuple-element.605, f32[1024]{0:T(1024)S(1)} %bitcast.127, bf16[511,1024]{1,0:T(8,128)(2,1)S(1)} %get-tuple-element.679, s32[]{:T(128)S(6)} %select_n.1433, f32[1024]{0:T(1024)S(1)} %bitcast.128, s32[]{:T(128)S(6)} %select_n.1434, ...), kind=kLoop, calls=%fused_computation.26.clone.1 | loop fusion | flops 33816576 | bytes 19013760 | tf_op jit(solution)/shard_map/while/body/eval_jaxpr/add | solution.py:46
  132.6 12.3 %select_add_fusion.3 = f32[256,1024]{1,0:T(8,128)S(1)} fusion(f32[256,1024]{1,0:T(8,128)S(1)} %get-tuple-element.605, f32[1024]{0:T(1024)S(1)} %bitcast.127, bf16[511,1024]{1,0:T(8,128)(2,1)S(1)} %get-tuple-element.679, s32[]{:T(128)S(6)} %select_n.1433, f32[1024]{0:T(1024)S(1)} %bitcast.128, s32[]{:T(128)S(6)} %select_n.1434, ...), kind=kLoop, calls=%fused_computation.26.clone.1 | loop fusion | flops 33816576 | bytes 19013760 | tf_op jit(solution)/shard_map/while/body/eval_jaxpr/add | solution.py:46
  148.4 12.3 %select_add_fusion.3 = f32[256,1024]{1,0:T(8,128)S(1)} fusion(f32[256,1024]{1,0:T(8,128)S(1)} %get-tuple-element.605, f32[1024]{0:T(1024)S(1)} %bitcast.127, bf16[511,1024]{1,0:T(8,128)(2,1)S(1)} %get-tuple-element.679, s32[]{:T(128)S(6)} %select_n.1433, f32[1024]{0:T(1024)S(1)} %bitcast.128, s32[]{:T(128)S(6)} %select_n.1434, ...), kind=kLoop, calls=%fused_computation.26.clone.1 | loop fusion | flops 33816576 | bytes 19013760 | tf_op jit(solution)/shard_map/while/body/eval_jaxpr/add | solution.py:46
  162.6 3.9 %fusion.28 = f32[256,1024]{1,0:T(8,128)} fusion(bf16[1,1024,1024]{2,1,0:T(8,128)(2,1)} %all-gather.7.cloned.1.call-done, f32[1024]{0:T(1024)S(1)} %bitcast.163, f32[256]{0:T(256)S(1)} %add_rsqrt_fusion.1, f32[256,1024]{1,0:T(8,128)S(1)} %get-tuple-element.276, f32[511,1024]{1,0:T(8,128)} %copy-done), kind=kOutput, calls=%fused_computation.95 | convolution fusion | flops 537919488 | bytes 5248000 | tf_op jit(solution)/shard_map/dot_general | solution.py:56
  166.5 4.9 %fusion.36 = bf16[256,1024]{1,0:T(8,128)(2,1)} fusion(bf16[1,1024,1024]{2,1,0:T(8,128)(2,1)} %all-gather.11.cloned.1.call-done, bf16[1,1024,1024]{2,1,0:T(8,128)(2,1)} %all-gather.9.cloned.1.call-done, f32[256,1024]{1,0:T(8,128)} %fusion.28, f32[1024]{0:T(1024)S(1)} %bitcast.164, f32[256]{0:T(256)S(1)} %add_rsqrt_fusion.1, ...), kind=kOutput, calls=%fused_computation.101 | convolution fusion | flops 1077149696 | bytes 9966592 | tf_op jit(solution)/shard_map/dot_general | solution.py:68
  (73 shorter events, 26.3 us)
Async XLA Ops:
  6.5 10.1 %copy-start.3 = (bf16[2,1024]{1,0:T(2,128)(2,1)S(1)}, bf16[2,1024]{1,0:T(2,128)(2,1)}, u32[]{:S(2)}) copy-start(bf16[2,1024]{1,0:T(2,128)(2,1)} %param.13) | copy-start | bytes 12292
  6.5 16.6 %copy-start.2 = (s32[256]{0:T(256)S(1)}, s32[256]{0:T(256)}, u32[]{:S(2)}) copy-start(s32[256]{0:T(256)} %param.11) | copy-start | bytes 3076
  6.5 156.0 %all-gather.7.cloned.1.call-start = ((), (), s32[]{:S(2)}) async-start(), calls=%async_computation | async-start | bytes 2359296 | tf_op jit(solution)/shard_map/all_gather | solution.py:58
  7.3 159.2 %all-gather.11.cloned.1.call-start = ((), (), s32[]{:S(2)}) async-start(), calls=%async_computation.2 | async-start | bytes 2359296 | tf_op jit(solution)/shard_map/all_gather | solution.py:70
  8.0 158.5 %all-gather.9.cloned.1.call-start = ((), (), s32[]{:S(2)}) async-start(), calls=%async_computation.1 | async-start | bytes 2359296 | tf_op jit(solution)/shard_map/all_gather | solution.py:63
  8.1 8.6 %collective-permute-start.1 = (bf16[2,1024]{1,0:T(2,128)(2,1)}, bf16[2,1024]{1,0:T(2,128)(2,1)S(1)}, u32[]{:S(2)}, u32[]{:S(2)}) collective-permute-start(bf16[2,1024]{1,0:T(2,128)(2,1)} %param.13), channel_id=1, source_target_pairs={{0,1},{1,0},{2,3},{3,2},{4,5},{5,4},{6,7},{7,6},{8,9},{9,8},{10,11... | collective-permute-start | bytes 12296 | tf_op jit(solution)/shard_map/ppermute | solution.py:93
  9.6 8.8 %collective-permute-start = (s32[256]{0:T(256)}, s32[256]{0:T(256)S(1)}, u32[]{:S(2)}, u32[]{:S(2)}) collective-permute-start(s32[256]{0:T(256)} %param.11), channel_id=1, source_target_pairs={{0,1},{1,2},{2,3},{3,4},{4,5},{5,6},{6,7},{7,8},{8,9},{9,10},{10,1... | collective-permute-start | bytes 3080 | tf_op jit(solution)/shard_map/ppermute | solution.py:13
  16.7 3.7 %collective-permute-start.2 = (bf16[4,1024]{1,0:T(4,128)(2,1)S(1)}, bf16[4,1024]{1,0:T(4,128)(2,1)S(1)}, u32[]{:S(2)}, u32[]{:S(2)}) collective-permute-start(bf16[4,1024]{1,0:T(4,128)(2,1)S(1)} %maximum_select_fusion.4), channel_id=1, source_target_pairs={{0,2},{1,3},{2,0},{3,1},{4,6},{5,7},{6,4},{7,5},{8,10},{9,11},{10,... | collective-permute-start | bytes 24584 | tf_op jit(solution)/shard_map/ppermute | solution.py:93
  20.5 5.1 %collective-permute-start.3 = (bf16[8,1024]{1,0:T(8,128)(2,1)S(1)}, bf16[8,1024]{1,0:T(8,128)(2,1)S(1)}, u32[]{:S(2)}, u32[]{:S(2)}) collective-permute-start(bf16[8,1024]{1,0:T(8,128)(2,1)S(1)} %maximum_select_fusion.3), channel_id=1, source_target_pairs={{0,4},{1,5},{2,6},{3,7},{4,0},{5,1},{6,2},{7,3},{8,12},{9,13},{10,... | collective-permute-start | bytes 49160 | tf_op jit(solution)/shard_map/ppermute | solution.py:93
  25.5 1.3 collective-permute-start.4
  26.8 4.3 %collective-permute-start.5 = (bf16[32,1024]{1,0:T(8,128)(2,1)S(1)}, bf16[32,1024]{1,0:T(8,128)(2,1)S(1)}, u32[]{:S(2)}, u32[]{:S(2)}) collective-permute-start(bf16[32,1024]{1,0:T(8,128)(2,1)S(1)} %maximum_select_fusion.1), channel_id=1, source_target_pairs={{0,16},{1,17},{2,18},{3,19},{4,20},{5,21},{6,22},{7,23},{8,24},{9,... | collective-permute-start | bytes 196616 | tf_op jit(solution)/shard_map/ppermute | solution.py:93
  160.9 1.3 copy-start
  162.5 3.9 %copy-start.1 = (f32[511,1024]{1,0:T(8,128)S(1)}, f32[511,1024]{1,0:T(8,128)}, u32[]{:S(2)}) copy-start(f32[511,1024]{1,0:T(8,128)} %copy-done) | copy-start | bytes 6279172
Sparse Core Ops, SparseCore 0:
  9.5 50.7 all-gather.6
  62.4 47.6 all-gather.10
  112.2 47.6 all-gather.8
